TPU v7x, 256 devices: a whole 4x4x8 slice. The times are simulated.
256 devices in a mesh: dp: 4 (over y), brick: 64 (over z, x, core).
Axes of the slice: x: 4, y: 4, z: 8, core: 2. Of those that a mesh axis runs over, the one named last changes fastest.
Arguments:
- features: bfloat16 [4, 512, 512, 64], P('dp', 'brick'), may hold values from -6 to 6
- occupancy: int32 [4, 512, 512], P('dp', 'brick'), may hold values 0 or 1
- neighbours: int32 [4, 512, 27], P('dp', 'brick'), may hold values from -1 to 511, as said below
- owners: int32 [4, 512], P('dp', 'brick'), may hold values from 0 to 511, as said below
- w_conv: bfloat16 [3, 3, 3, 64, 64], replicated, may hold values from -0.15625 to 0.15625
- w_down: bfloat16 [2, 2, 2, 64, 128], replicated, may hold values from -0.25 to 0.25
- w_point: bfloat16 [128, 256], replicated, may hold values from -0.5 to 0.5
- cotangent: bfloat16 [4, 512, 64, 256], P('dp', 'brick'), may hold values from -0.015625 to 0.015625
Outputs:
- grad_w_conv: float32 [3, 3, 3, 64, 64], replicated
- grad_w_down: float32 [2, 2, 2, 64, 128], replicated
- grad_w_point: float32 [128, 256], replicated
Inputs may be any that keep to these rules, and one draw needn't show every extreme that they name: `neighbours`: bricks of a scene form a lattice of 128 x 4 x 1 bricks, 8 consecutive ids a device; an entry names the lattice neighbour at its column's offset or is -1; column 13 is the brick itself. Columns with first offset 0 name bricks of the same device, offset -1 of the same or the previous device, offset +1 of the same or the next. `owners`: within a scene a permutation of the coarse slots; a slot's device is slot // 8. A device hands exactly 1 bricks to each device it hands any to.
All inputs are finite; a program needn't handle non-finite values. No bound on the sum of `occupancy` on one device may be relied on, other than what follows from the above.
Results may differ from a plain program's by a relative error of at most 0.012.
Values may be sent and summed in bfloat16 or wider, within the bound.
A program may use at most 64 MiB of HBM per device.

v0:
```python
import jax
import jax.numpy as jnp
from jax import lax
from jax.sharding import PartitionSpec as P

SPANS = ((7, 8), (0, 8), (0, 1))


def extended(shard, sides, width):
    for axis, dim in sides:
        peers, length = (lax.axis_size(axis), shard.shape[dim])
        up = [(i, (i + 1) % peers) for i in range(peers - 1)]
        down = [(j, i) for i, j in up]
        last = lax.slice_in_dim(shard, length - width, length, axis=dim)
        initial = lax.slice_in_dim(shard, 0, width, axis=dim)
        before = lax.ppermute(last, axis, up)
        after = lax.ppermute(initial, axis, down)
        shard = jnp.concatenate([before, shard, after], axis=dim)
    return shard


def assemble(pools, indices):
    planes = []
    for a in range(3):
        row_parts = []
        for b in range(3):
            col_parts = []
            for c in range(3):
                window_part = pools[a][
                    :, :, SPANS[b][0] : SPANS[b][1], SPANS[c][0] : SPANS[c][1], :
                ]
                col_parts.append(
                    jnp.take(window_part, indices[a][:, 9 * a + 3 * b + c], axis=0, mode="clip")
                )
            row_parts.append(jnp.concatenate(col_parts, axis=3))
        planes.append(jnp.concatenate(row_parts, axis=2))
    return jnp.concatenate(planes, axis=1)


def silu_slope(signal):
    gate_value = jax.nn.sigmoid(signal)
    return gate_value * (1.0 + signal * (1.0 - gate_value))


def point_layer(rows_in, cot_rows, w_point):
    brick_count = rows_in.shape[0]
    row_block = rows_in.reshape(-1, w_point.shape[0])
    point_act = jnp.dot(row_block, w_point, preferred_element_type=jnp.float32)
    grad_point = (
        cot_rows.reshape(point_act.shape).astype(jnp.float32) * silu_slope(point_act)
    ).astype(jnp.bfloat16)
    grad_weight = lax.dot_general(
        row_block, grad_point, (((0,), (0,)), ((), ())), preferred_element_type=jnp.float32
    )
    grad_rows = lax.dot_general(
        grad_point, w_point, (((1,), (1,)), ((), ())), preferred_element_type=jnp.float32
    )
    return (grad_rows.astype(jnp.bfloat16).reshape(brick_count, -1), grad_weight)


def shards(features, occupancy, neighbours, owners, w_conv, w_down, w_point, cotangent):
    brick_count = features.shape[1]
    in_width = features.shape[3]
    brick_devices = lax.axis_size("brick")
    device_pos = lax.axis_index("brick")
    bricks = features[0].reshape(brick_count, 8, 8, 8, in_width)
    link_table = neighbours[0]
    linked = link_table >= 0
    local_ids = link_table - device_pos * brick_count
    zero_brick = jnp.zeros((1, 8, 8, 8, in_width), bricks.dtype)
    beside_all = extended(bricks, (("brick", 0),), brick_count)
    brick_pool = jnp.concatenate([beside_all, zero_brick], axis=0)
    pool_index = jnp.where(linked, local_ids + brick_count, 3 * brick_count)
    padded = assemble(
        (brick_pool[:, 7:8], brick_pool, brick_pool[:, 0:1]), (pool_index, pool_index, pool_index)
    )
    pre_act = lax.conv_general_dilated(
        padded,
        w_conv,
        (1, 1, 1),
        "VALID",
        dimension_numbers=("NDHWC", "DHWIO", "NDHWC"),
        preferred_element_type=jnp.float32,
    )
    occupied = occupancy[0].reshape(brick_count, 8, 8, 8, 1).astype(jnp.float32)
    hidden = (jax.nn.silu(pre_act) * occupied).astype(jnp.bfloat16)
    grouped = hidden.reshape(brick_count, 4, 2, 4, 2, 4, 2, in_width)
    down_act = jnp.einsum(
        "bpiqjrkc,ijkcd->bpqrd", grouped, w_down, preferred_element_type=jnp.float32
    )
    coarse = jax.nn.silu(down_act).astype(jnp.bfloat16).reshape(brick_count, -1)
    target_dev = owners[0] // brick_count
    recv_slot = owners[0] % brick_count
    capacity = max(1, brick_count // brick_devices)
    dest_hits = (target_dev[:, None] == jnp.arange(brick_devices, dtype=jnp.int32)[None, :]).astype(
        jnp.int32
    )
    earlier_hits = jnp.cumsum(dest_hits, axis=0) - dest_hits
    rank_in = jnp.sum(earlier_hits * dest_hits, axis=1)
    position = target_dev * capacity + rank_in
    slot_out = jnp.full((brick_devices * capacity,), -1, jnp.int32).at[position].set(recv_slot)
    arrived = lax.all_to_all(slot_out, "brick", split_axis=0, concat_axis=0, tiled=True)
    present = arrived >= 0
    safe_slots = jnp.where(present, arrived, 0)
    send_rows = (
        jnp.zeros((brick_devices * capacity, coarse.shape[1]), jnp.bfloat16)
        .at[position]
        .set(coarse)
    )
    landed = lax.all_to_all(send_rows, "brick", split_axis=0, concat_axis=0, tiled=True)
    drop_slots = jnp.where(present, arrived, brick_count)
    placed = jnp.zeros_like(coarse).at[drop_slots].set(landed, mode="drop")
    grad_placed, grad_w_point = point_layer(placed, cotangent[0], w_point)
    reply = jnp.where(
        present[:, None], jnp.take(grad_placed, safe_slots, axis=0), jnp.zeros((), jnp.bfloat16)
    )
    returned = lax.all_to_all(reply, "brick", split_axis=0, concat_axis=0, tiled=True)
    grad_coarse = jnp.take(returned, position, axis=0)
    grad_down = (
        grad_coarse.reshape(down_act.shape).astype(jnp.float32) * silu_slope(down_act)
    ).astype(jnp.bfloat16)
    grad_w_down = jnp.einsum(
        "bpiqjrkc,bpqrd->ijkcd", grouped, grad_down, preferred_element_type=jnp.float32
    )
    grad_hidden = jnp.einsum(
        "bpqrd,ijkcd->bpiqjrkc", grad_down, w_down, preferred_element_type=jnp.float32
    )
    grad_hidden = grad_hidden.reshape(brick_count, 8, 8, 8, in_width)
    grad_pre = (grad_hidden * occupied * silu_slope(pre_act)).astype(jnp.bfloat16)
    flat_grad = grad_pre.reshape(-1, in_width)
    term_list = []
    for a in range(3):
        for b in range(3):
            for c in range(3):
                window_part = padded[:, a : a + 8, b : b + 8, c : c + 8, :].reshape(-1, in_width)
                term_list.append(
                    lax.dot_general(
                        window_part,
                        flat_grad,
                        (((0,), (0,)), ((), ())),
                        preferred_element_type=jnp.float32,
                    )
                )
    grad_w_conv = jnp.stack(term_list).reshape(3, 3, 3, in_width, in_width)
    summed = lax.psum((grad_w_conv, grad_w_down, grad_w_point), ("dp", "brick"))
    return (summed[0], summed[1], summed[2])


def solution(mesh):
    in_specs = (
        P("dp", "brick", None, None),
        P("dp", "brick", None),
        P("dp", "brick", None),
        P("dp", "brick"),
        P(),
        P(),
        P(),
        P("dp", "brick", None, None),
    )
    out_specs = (P(), P(), P())
    return jax.shard_map(shards, mesh=mesh, in_specs=in_specs, out_specs=out_specs, check_vma=False)
```

profile of v0, /device:TPU:97, one launch (start us, length us, event | category | flops | bytes accessed | tf_op | source)
XLA Modules:
  0.0 517.1 jit_solution(3569445359638503586)
XLA Ops:
  7.2 1.9 copy.274
  9.1 3.7 collective-permute-start
  12.7 1.9 collective-permute-start.1
  17.6 11.8 %all-to-all-start = ((s32[64,1,1]{2,1,0:T(1,128)}), s32[64,1,1]{2,1,0:T(1,128)S(1)}, u32[]{:S(2)}, u32[]{:S(2)}) async-start(s32[64,1,1]{2,1,0:T(1,128)} %copy.303), calls=%async_computation | async-start | bytes 65536 | tf_op jit(solution)/shard_map/all_to_all | solution.py:102
  40.4 1.2 reduce.18
  42.8 2.9 maximum_maximum_fusion
  48.7 3.0 copy.293
  51.7 0.9 copy.294
  52.6 1.6 gather_fusion.14
  54.3 0.9 copy.291
  55.2 1.6 gather_fusion.12
  75.9 2.8 gather_fusion.13
  78.7 1.2 copy.296
  80.6 2.1 gather_fusion.7
  82.7 1.3 copy.422
  84.0 1.5 copy.281
  85.5 2.1 gather_fusion.5
  87.6 1.3 copy.423
  88.9 1.5 copy.277
  90.4 2.1 gather_fusion.3
  92.4 1.3 copy.424
  94.4 1.5 gather_fusion.1
  95.9 0.9 copy.279
  96.8 1.7 gather_fusion.4
  98.6 1.4 gather_fusion.8
  100.1 1.4 gather_fusion.18
  101.5 1.4 gather_fusion.20
  102.8 1.4 gather_fusion.24
  104.2 1.4 gather_fusion.26
  105.6 1.4 gather_fusion.6
  107.0 1.4 gather_fusion.2
  108.4 1.4 gather_fusion
  109.8 6.8 %multiply_convert_fusion.1 = (bf16[8,8,8,8,64]{4,0,3,2,1:T(8,128)(2,1)S(1)}, f32[8,8,8,8,64]{4,0,3,2,1:T(8,128)}) fusion(f32[8,8,8,8]{0,3,2,1:T(8,128)} %bitcast.539, bf16[3,3,3,64,64]{4,3,2,1,0:T(8,128)(2,1)S(1)} %copy-done, bf16[8,1,1,1,64]{4,0,3,2,1:T(8,128)(2,1)S(1)} %bitcast.601, bf16[8,1,1,8,64]{4,0,3,2,1:T(8,128)(2,1)} %bitcast.573, ...), kind=kOutput, calls=%fused_computation.34 | convolution fusion | flops 920854528 | bytes 2834432 | tf_op jit(solution)/shard_map/conv_general_dilated | solution.py:77
  117.8 1.5 scatter_custom_fusion.1
  119.8 2.1 reduce.56
  121.9 2.6 reshape.781
  124.5 10.3 %all-to-all-start.1 = ((bf16[64,2,4096]{2,1,0:T(2,128)(2,1)}), bf16[64,2,4096]{2,1,0:T(2,128)(2,1)S(1)}, u32[]{:S(2)}, u32[]{:S(2)}) async-start(bf16[64,2,4096]{2,1,0:T(2,128)(2,1)} %reshape.781), calls=%async_computation.1 | async-start | bytes 2097152 | tf_op jit(solution)/shard_map/all_to_all | solution.py:110
  134.9 26.5 %all-to-all-done.1 = bf16[64,2,4096]{2,1,0:T(2,128)(2,1)S(1)} async-done(((bf16[64,2,4096]{2,1,0:T(2,128)(2,1)}), bf16[64,2,4096]{2,1,0:T(2,128)(2,1)S(1)}, u32[]{:S(2)}, u32[]{:S(2)}) %all-to-all-start.1) | async-done | bytes 1048608 | tf_op jit(solution)/shard_map/all_to_all | solution.py:110
  161.4 3.5 reshape.782
  164.9 4.0 scatter_custom_fusion.2
  169.7 1.3 fusion.92
  171.3 1.3 gather_fusion.27
  172.6 1.2 fusion.86
  173.8 2.7 reduce.57
  176.5 1.6 reshape.783
  178.1 7.9 %all-to-all-start.2 = ((bf16[64,2,4096]{2,1,0:T(2,128)(2,1)}), bf16[64,2,4096]{2,1,0:T(2,128)(2,1)S(1)}, u32[]{:S(2)}, u32[]{:S(2)}) async-start(bf16[64,2,4096]{2,1,0:T(2,128)(2,1)} %reshape.783), calls=%async_computation.2 | async-start | bytes 2097152 | tf_op jit(solution)/shard_map/all_to_all | solution.py:117
  186.0 1.3 pad_clamp_fusion
  187.3 1.2 compare_and_fusion.1
  188.5 0.9 copy.319
  189.5 0.9 copy.322
  190.5 6.2 %maximum_maximum_fusion.2 = bf16[8,9,10,10,64]{4,0,3,2,1:T(8,128)(2,1)} fusion(bf16[8,1,1,1,64]{4,0,3,2,1:T(8,128)(2,1)} %bitcast.602, bf16[8,1,1,8,64]{4,0,3,2,1:T(8,128)(2,1)S(1)} %bitcast.574, bf16[8,1,1,1,64]{4,0,3,2,1:T(8,128)(2,1)} %bitcast.598, bf16[8,1,8,1,64]{4,0,3,2,1:T(8,128)(2,1)S(1)} %bitcast.576, bf16[8,1,8,8,64]{4,0,3,2,1:T(8,128)(2,1)S(1)} %bitcast.545, ...), kind=kLoop, calls=%fused_computation.91 | loop fusion | flops 7833600 | bytes 1843200 | tf_op jit(solution)/shard_map/concatenate | solution.py:37
  196.7 3.3 maximum_maximum_fusion.1
  200.9 11.7 %all-to-all-done.2 = bf16[64,2,4096]{2,1,0:T(2,128)(2,1)S(1)} async-done(((bf16[64,2,4096]{2,1,0:T(2,128)(2,1)}), bf16[64,2,4096]{2,1,0:T(2,128)(2,1)S(1)}, u32[]{:S(2)}, u32[]{:S(2)}) %all-to-all-start.2) | async-done | bytes 1048608 | tf_op jit(solution)/shard_map/all_to_all | solution.py:117
  212.6 3.5 reshape.784
  216.1 2.8 copy.406
  219.6 1.8 convolution_bitcast_fusion.1
  222.9 1.3 copy-done.3
  224.2 1.1 multiply_convert_fusion
  234.5 1.0 fusion.72
  237.1 1.0 copy-done.4
  242.8 0.9 copy-done.12
  243.7 261.8 %all-reduce.3.cloned.1.call-done = (f32[3,3,3,64,64]{4,3,2,1,0:T(8,128)}, f32[2,2,2,64,128]{4,3,0,1,2:T(8,128)}, f32[128,256]{1,0:T(8,128)}) async-done(((f32[3,3,3,64,64]{4,3,2,1,0:T(8,128)}, f32[2,2,2,64,128]{4,3,0,1,2:T(8,128)}, f32[128,256]{1,0:T(8,128)}), (f32[3,3,3,64,64]{4,3,2,1,0:T(8,128)}, f32[2,2,2,64,128]{4,3,0,1,2:T(8,128)}, f32[128,256]{1,0:T(8,128)})) %all-reduce.3.cloned.1.call-update) | async-done | bytes 835600 | tf_op jit(solution)/shard_map/psum | solution.py:145
  505.5 1.7 copy.325
  507.2 2.2 copy.457
  (224 shorter events, 60.4 us)
Async XLA Ops:
  7.2 102.6 %copy-start = (bf16[3,3,3,64,64]{4,3,2,1,0:T(8,128)(2,1)S(1)}, bf16[3,3,3,64,64]{4,3,2,1,0:T(8,128)(2,1)}, u32[]{:S(2)}) copy-start(bf16[3,3,3,64,64]{4,3,2,1,0:T(8,128)(2,1)} %param.12) | copy-start | bytes 663556
  9.1 33.8 %collective-permute-start = (bf16[8,8,8,8,64]{4,0,3,2,1:T(8,128)(2,1)S(1)}, bf16[8,8,8,8,64]{4,0,3,2,1:T(8,128)(2,1)S(1)}, u32[]{:S(2)}, u32[]{:S(2)}) collective-permute-start(bf16[8,8,8,8,64]{4,0,3,2,1:T(8,128)(2,1)S(1)} %bitcast.503), channel_id=1, source_target_pairs={{0,1},{1,2},{2,3},{3,4},{4,5},{5,6},{6,7},{7,8},{8,9},{9,10},{10,1... | collective-permute-start | bytes 1572872 | tf_op jit(solution)/shard_map/ppermute | solution.py:16
  12.7 30.1 %collective-permute-start.1 = (bf16[8,8,8,8,64]{4,0,3,2,1:T(8,128)(2,1)S(1)}, bf16[8,8,8,8,64]{4,0,3,2,1:T(8,128)(2,1)}, u32[]{:S(2)}, u32[]{:S(2)}) collective-permute-start(bf16[8,8,8,8,64]{4,0,3,2,1:T(8,128)(2,1)S(1)} %bitcast.504), channel_id=1, source_target_pairs={{1,0},{2,1},{3,2},{4,3},{5,4},{6,5},{7,6},{8,7},{9,8},{10,9},{11,1... | collective-permute-start | bytes 1572872 | tf_op jit(solution)/shard_map/ppermute | solution.py:17
  15.3 2.3 copy-start.47
  15.6 2.0 copy-start.50
  16.3 1.3 copy-start.51
  17.6 22.8 %all-to-all-start = ((s32[64,1,1]{2,1,0:T(1,128)}), s32[64,1,1]{2,1,0:T(1,128)S(1)}, u32[]{:S(2)}, u32[]{:S(2)}) async-start(s32[64,1,1]{2,1,0:T(1,128)} %copy.303), calls=%async_computation | async-start | bytes 65536 | tf_op jit(solution)/shard_map/all_to_all | solution.py:102
  41.6 4.1 copy-start.48
  58.3 14.6 %copy-start.21 = (bf16[25,8,64]{2,0,1:T(8,128)(2,1)S(1)}, bf16[25,8,64]{2,0,1:T(8,128)(2,1)}, u32[]{:S(2)}) copy-start(bf16[25,8,64]{2,0,1:T(8,128)(2,1)} %get-tuple-element.47) | copy-start | bytes 76804
  64.9 44.9 %copy-start.6 = (bf16[8,8,8,64]{3,0,2,1:T(8,128)(2,1)}, bf16[8,8,8,64]{3,0,2,1:T(8,128)(2,1)S(1)}, u32[]{:S(2)}) copy-start(bf16[8,8,8,64]{3,0,2,1:T(8,128)(2,1)S(1)} %copy.409) | copy-start | bytes 196612
  78.7 20.0 %copy-start.1 = (bf16[8,8,8,8,64]{4,3,2,1,0:T(8,128)(2,1)}, bf16[8,8,8,8,64]{4,3,2,1,0:T(8,128)(2,1)S(1)}, u32[]{:S(2)}) copy-start(bf16[8,8,8,8,64]{4,3,2,1,0:T(8,128)(2,1)S(1)} %gather_fusion.13) | copy-start | bytes 1572868
  78.7 1.3 copy-start.20
  95.9 20.7 %copy-start.32 = (bf16[8,8,64]{2,0,1:T(8,128)(2,1)}, bf16[8,8,64]{2,0,1:T(8,128)(2,1)S(1)}, u32[]{:S(2)}) copy-start(bf16[8,8,64]{2,0,1:T(8,128)(2,1)S(1)} %copy.425) | copy-start | bytes 24580
  98.6 18.0 %copy-start.14 = (bf16[8,8,8,64]{3,0,2,1:T(8,128)(2,1)}, bf16[8,8,8,64]{3,0,2,1:T(8,128)(2,1)S(1)}, u32[]{:S(2)}) copy-start(bf16[8,8,8,64]{3,0,2,1:T(8,128)(2,1)S(1)} %copy.413) | copy-start | bytes 196612
  100.1 16.6 %copy-start.35 = (bf16[8,64]{1,0:T(8,128)(2,1)}, bf16[8,64]{1,0:T(8,128)(2,1)S(1)}, u32[]{:S(2)}) copy-start(bf16[8,64]{1,0:T(8,128)(2,1)S(1)} %gather_fusion.8) | copy-start | bytes 3076
  101.4 15.2 %copy-start.37 = (bf16[8,64]{1,0:T(8,128)(2,1)}, bf16[8,64]{1,0:T(8,128)(2,1)S(1)}, u32[]{:S(2)}) copy-start(bf16[8,64]{1,0:T(8,128)(2,1)S(1)} %gather_fusion.18) | copy-start | bytes 3076
  102.8 13.8 %copy-start.38 = (bf16[8,64]{1,0:T(8,128)(2,1)}, bf16[8,64]{1,0:T(8,128)(2,1)S(1)}, u32[]{:S(2)}) copy-start(bf16[8,64]{1,0:T(8,128)(2,1)S(1)} %gather_fusion.20) | copy-start | bytes 3076
  104.2 12.4 %copy-start.41 = (bf16[8,64]{1,0:T(8,128)(2,1)}, bf16[8,64]{1,0:T(8,128)(2,1)S(1)}, u32[]{:S(2)}) copy-start(bf16[8,64]{1,0:T(8,128)(2,1)S(1)} %gather_fusion.24) | copy-start | bytes 3076
  105.6 11.0 %copy-start.44 = (bf16[8,64]{1,0:T(8,128)(2,1)}, bf16[8,64]{1,0:T(8,128)(2,1)S(1)}, u32[]{:S(2)}) copy-start(bf16[8,64]{1,0:T(8,128)(2,1)S(1)} %gather_fusion.26) | copy-start | bytes 3076
  107.0 9.6 %copy-start.39 = (bf16[8,64]{1,0:T(8,128)(2,1)}, bf16[8,64]{1,0:T(8,128)(2,1)S(1)}, u32[]{:S(2)}) copy-start(bf16[8,64]{1,0:T(8,128)(2,1)S(1)} %gather_fusion.6) | copy-start | bytes 3076
  108.4 8.3 %copy-start.42 = (bf16[8,64]{1,0:T(8,128)(2,1)}, bf16[8,64]{1,0:T(8,128)(2,1)S(1)}, u32[]{:S(2)}) copy-start(bf16[8,64]{1,0:T(8,128)(2,1)S(1)} %gather_fusion.2) | copy-start | bytes 3076
  109.8 6.9 %copy-start.45 = (bf16[8,64]{1,0:T(8,128)(2,1)}, bf16[8,64]{1,0:T(8,128)(2,1)S(1)}, u32[]{:S(2)}) copy-start(bf16[8,64]{1,0:T(8,128)(2,1)S(1)} %gather_fusion) | copy-start | bytes 3076
  109.8 6.9 %copy-start.24 = (bf16[2,2,2,64,128]{4,3,2,1,0:T(8,128)(2,1)S(1)}, bf16[2,2,2,64,128]{4,3,2,1,0:T(8,128)(2,1)}, u32[]{:S(2)}) copy-start(bf16[2,2,2,64,128]{4,3,2,1,0:T(8,128)(2,1)} %param.13) | copy-start | bytes 393220
  116.7 1.0 copy-start.53
  117.1 0.7 copy-start.9
  121.9 12.9 %copy-start.49 = (s32[64]{0:T(128)S(1)}, s32[64]{0:T(128)}, u32[]{:S(2)}) copy-start(s32[64]{0:T(128)} %copy-done.48) | copy-start | bytes 772
  124.5 36.9 %all-to-all-start.1 = ((bf16[64,2,4096]{2,1,0:T(2,128)(2,1)}), bf16[64,2,4096]{2,1,0:T(2,128)(2,1)S(1)}, u32[]{:S(2)}, u32[]{:S(2)}) async-start(bf16[64,2,4096]{2,1,0:T(2,128)(2,1)} %reshape.781), calls=%async_computation.1 | async-start | bytes 2097152 | tf_op jit(solution)/shard_map/all_to_all | solution.py:110
  134.9 34.8 %copy-start.34 = (bf16[128,256]{1,0:T(8,128)(2,1)S(1)}, bf16[128,256]{1,0:T(8,128)(2,1)}, u32[]{:S(2)}) copy-start(bf16[128,256]{1,0:T(8,128)(2,1)} %param.14) | copy-start | bytes 196612
  169.0 0.6 copy-start.16
  176.4 14.0 %copy-start.7 = (bf16[8,8,8,64]{3,0,2,1:T(8,128)(2,1)S(1)}, bf16[8,8,8,64]{3,0,2,1:T(8,128)(2,1)}, u32[]{:S(2)}) copy-start(bf16[8,8,8,64]{3,0,2,1:T(8,128)(2,1)} %copy-done.6) | copy-start | bytes 196612
  176.5 14.0 %copy-start.8 = (bf16[8,8,8,64]{3,0,2,1:T(8,128)(2,1)S(1)}, bf16[8,8,8,64]{3,0,2,1:T(8,128)(2,1)}, u32[]{:S(2)}) copy-start(bf16[8,8,8,64]{3,0,2,1:T(8,128)(2,1)} %copy.412) | copy-start | bytes 196612
  176.5 14.0 %copy-start.13 = (bf16[8,8,8,64]{3,0,2,1:T(8,128)(2,1)S(1)}, bf16[8,8,8,64]{3,0,2,1:T(8,128)(2,1)}, u32[]{:S(2)}) copy-start(bf16[8,8,8,64]{3,0,2,1:T(8,128)(2,1)} %copy.408) | copy-start | bytes 196612
  176.5 13.9 %copy-start.22 = (bf16[8,8,64]{2,0,1:T(8,128)(2,1)S(1)}, bf16[8,8,64]{2,0,1:T(8,128)(2,1)}, u32[]{:S(2)}) copy-start(bf16[8,8,64]{2,0,1:T(8,128)(2,1)} %copy.420) | copy-start | bytes 24580
  176.5 13.9 %copy-start.23 = (bf16[8,8,64]{2,0,1:T(8,128)(2,1)S(1)}, bf16[8,8,64]{2,0,1:T(8,128)(2,1)}, u32[]{:S(2)}) copy-start(bf16[8,8,64]{2,0,1:T(8,128)(2,1)} %copy.421) | copy-start | bytes 24580
  176.5 13.9 %copy-start.27 = (bf16[8,8,64]{2,0,1:T(8,128)(2,1)S(1)}, bf16[8,8,64]{2,0,1:T(8,128)(2,1)}, u32[]{:S(2)}) copy-start(bf16[8,8,64]{2,0,1:T(8,128)(2,1)} %copy.414) | copy-start | bytes 24580
  176.5 13.9 %copy-start.28 = (bf16[8,8,64]{2,0,1:T(8,128)(2,1)S(1)}, bf16[8,8,64]{2,0,1:T(8,128)(2,1)}, u32[]{:S(2)}) copy-start(bf16[8,8,64]{2,0,1:T(8,128)(2,1)} %copy.415) | copy-start | bytes 24580
  178.1 34.5 %all-to-all-start.2 = ((bf16[64,2,4096]{2,1,0:T(2,128)(2,1)}), bf16[64,2,4096]{2,1,0:T(2,128)(2,1)S(1)}, u32[]{:S(2)}, u32[]{:S(2)}) async-start(bf16[64,2,4096]{2,1,0:T(2,128)(2,1)} %reshape.783), calls=%async_computation.2 | async-start | bytes 2097152 | tf_op jit(solution)/shard_map/all_to_all | solution.py:117
  186.0 319.5 %all-reduce.3.cloned.1.call-start = ((), (), s32[]{:S(2)}) async-start(), calls=%async_computation.3 | async-start | bytes 2555904 | tf_op jit(solution)/shard_map/psum | solution.py:145
  189.4 7.2 %copy-start.15 = (bf16[8,8,8,64]{3,0,2,1:T(8,128)(2,1)S(1)}, bf16[8,8,8,64]{3,0,2,1:T(8,128)(2,1)}, u32[]{:S(2)}) copy-start(bf16[8,8,8,64]{3,0,2,1:T(8,128)(2,1)} %copy-done.14) | copy-start | bytes 196612
  189.4 7.2 %copy-start.29 = (bf16[8,8,64]{2,0,1:T(8,128)(2,1)S(1)}, bf16[8,8,64]{2,0,1:T(8,128)(2,1)}, u32[]{:S(2)}) copy-start(bf16[8,8,64]{2,0,1:T(8,128)(2,1)} %copy.422) | copy-start | bytes 24580
  189.4 7.2 %copy-start.30 = (bf16[8,8,64]{2,0,1:T(8,128)(2,1)S(1)}, bf16[8,8,64]{2,0,1:T(8,128)(2,1)}, u32[]{:S(2)}) copy-start(bf16[8,8,64]{2,0,1:T(8,128)(2,1)} %copy.423) | copy-start | bytes 24580
  189.4 7.2 %copy-start.31 = (bf16[8,8,64]{2,0,1:T(8,128)(2,1)S(1)}, bf16[8,8,64]{2,0,1:T(8,128)(2,1)}, u32[]{:S(2)}) copy-start(bf16[8,8,64]{2,0,1:T(8,128)(2,1)} %copy.424) | copy-start | bytes 24580
  189.5 7.2 %copy-start.33 = (bf16[8,8,64]{2,0,1:T(8,128)(2,1)S(1)}, bf16[8,8,64]{2,0,1:T(8,128)(2,1)}, u32[]{:S(2)}) copy-start(bf16[8,8,64]{2,0,1:T(8,128)(2,1)} %copy-done.32) | copy-start | bytes 24580
  189.5 7.2 %copy-start.36 = (bf16[8,64]{1,0:T(8,128)(2,1)S(1)}, bf16[8,64]{1,0:T(8,128)(2,1)}, u32[]{:S(2)}) copy-start(bf16[8,64]{1,0:T(8,128)(2,1)} %copy-done.35) | copy-start | bytes 3076
  189.5 7.2 %copy-start.40 = (bf16[8,64]{1,0:T(8,128)(2,1)S(1)}, bf16[8,64]{1,0:T(8,128)(2,1)}, u32[]{:S(2)}) copy-start(bf16[8,64]{1,0:T(8,128)(2,1)} %copy-done.39) | copy-start | bytes 3076
  189.5 7.2 %copy-start.43 = (bf16[8,64]{1,0:T(8,128)(2,1)S(1)}, bf16[8,64]{1,0:T(8,128)(2,1)}, u32[]{:S(2)}) copy-start(bf16[8,64]{1,0:T(8,128)(2,1)} %copy-done.42) | copy-start | bytes 3076
  189.5 7.2 %copy-start.46 = (bf16[8,64]{1,0:T(8,128)(2,1)S(1)}, bf16[8,64]{1,0:T(8,128)(2,1)}, u32[]{:S(2)}) copy-start(bf16[8,64]{1,0:T(8,128)(2,1)} %copy-done.45) | copy-start | bytes 3076
  196.7 3.3 copy-start.17
  216.1 3.5 copy-start.10
  216.1 3.5 copy-start.52
  219.6 1.8 copy-start.25
  222.6 1.6 copy-start.3
  222.6 1.6 copy-start.11
  224.2 1.5 copy-start.5
  231.4 1.2 copy-start.2
  231.4 1.3 copy-start.19
  233.6 1.0 copy-start.18
  236.6 1.5 copy-start.4
  242.8 0.9 copy-start.12
  505.5 3.9 copy-start.26
Sparse Core Ops, SparseCore 0:
  243.8 261.6 all-reduce.2
where the time goes:
time: 523 us; the launch traced here: 517 us
  waiting for transfers between devices  300 us (57%)
  local copies, waits for them, and re-layouts  104 us (20%)
  starting transfers between devices  35.6 us (7%)
  other arithmetic  35.2 us (7%)
  matrix products  26.6 us (5%)
  between operations  15.2 us (3%)
    psum x1, waiting for transfers between devices, shards(): summed = lax.psum((grad_w_conv, grad_w_down, grad_w_point), ('dp', 'brick'))  262 us
    gather x48, local copies, waits for them, and re-layouts, assemble(): jnp.take(window_part, indices[a][:, 9 * a + 3 * b + c], axis=0, mode='clip')  46 us
    all_to_all x1, waiting for transfers between devices, shards(): lax.all_to_all(send_rows, 'brick', split_axis=0, concat_axis=0, tiled=True)  26.5 us
    unnamed x117, local copies, waits for them, and re-layouts  26.5 us
    slice x22, local copies, waits for them, and re-layouts, assemble(): pools[a][:, :, SPANS[b][0]:SPANS[b][1], SPANS[c][0]:SPANS[c][1], :]  15.4 us
    dot_general x27, matrix products, shards(): lax.dot_general(window_part, flat_grad, (((0,), (0,)), ((), ())), preferr...  14.9 us
    all_to_all x1, starting transfers between devices, shards(): lax.all_to_all(slot_out, 'brick', split_axis=0, concat_axis=0, tiled=True)  11.8 us
    all_to_all x1, waiting for transfers between devices, shards(): lax.all_to_all(reply, 'brick', split_axis=0, concat_axis=0, tiled=True)  11.7 us
  transfers between devices with their start and end apart: 6, of which 3 were waited for; matrix products, arithmetic and copies ran while one was open for 6% of the time, Pallas kernels for 0%

commit v1 on v0

--- a/solution.py
+++ b/solution.py
@@ -142,7 +142,7 @@
                     )
                 )
     grad_w_conv = jnp.stack(term_list).reshape(3, 3, 3, in_width, in_width)
-    summed = lax.psum((grad_w_conv, grad_w_down, grad_w_point), ("dp", "brick"))
+    summed = lax.psum(lax.psum((grad_w_conv, grad_w_down, grad_w_point), axis_name="dp"), "brick")
     return (summed[0], summed[1], summed[2])
 
 

time: 523 us -> 507 us (0.969)
  waiting for transfers between devices: 300 us -> 284 us
    psum x1 -> x2, waiting for transfers between devices: 262 us -> 246 us  [the longest x1 195 us: shards(): lax.psum(lax.psum((grad_w_conv, grad_w_down, grad_w_point), axis_name='dp...]
  transfers between devices with their start and end apart: 6 -> 7, of which waited for: 3 -> 4; matrix products, arithmetic and copies ran while one was open for 6% -> 6% of each run, Pallas kernels for 0% -> 0%
where the time goes in v1:
time: 507 us; the launch traced here: 501 us
  waiting for transfers between devices  284 us (56%)
  local copies, waits for them, and re-layouts  104 us (21%)
  starting transfers between devices  35.7 us (7%)
  other arithmetic  35.2 us (7%)
  matrix products  26.6 us (5%)
  between operations  15.3 us (3%)
    psum x1, waiting for transfers between devices, shards(): lax.psum(lax.psum((grad_w_conv, grad_w_down, grad_w_point), axis_name='dp...  195 us
    psum x1, waiting for transfers between devices, shards(): lax.psum((grad_w_conv, grad_w_down, grad_w_point), axis_name='dp')  50.9 us
    gather x48, local copies, waits for them, and re-layouts, assemble(): jnp.take(window_part, indices[a][:, 9 * a + 3 * b + c], axis=0, mode='clip')  46 us
    all_to_all x1, waiting for transfers between devices, shards(): lax.all_to_all(send_rows, 'brick', split_axis=0, concat_axis=0, tiled=True)  26.5 us
    unnamed x117, local copies, waits for them, and re-layouts  26.5 us
    slice x22, local copies, waits for them, and re-layouts, assemble(): pools[a][:, :, SPANS[b][0]:SPANS[b][1], SPANS[c][0]:SPANS[c][1], :]  15.4 us
    dot_general x27, matrix products, shards(): lax.dot_general(window_part, flat_grad, (((0,), (0,)), ((), ())), preferr...  14.9 us
    all_to_all x1, starting transfers between devices, shards(): lax.all_to_all(slot_out, 'brick', split_axis=0, concat_axis=0, tiled=True)  11.8 us
  transfers between devices with their start and end apart: 7, of which 4 were waited for; matrix products, arithmetic and copies ran while one was open for 6% of the time, Pallas kernels for 0%

profile of v1, /device:TPU:97, one launch (start us, length us, event | category | flops | bytes accessed | tf_op | source)
XLA Modules:
  0.0 501.0 jit_solution(14554308801052425694)
XLA Ops:
  7.2 1.9 copy.274
  9.1 3.7 collective-permute-start
  12.7 1.9 collective-permute-start.1
  17.6 11.8 %all-to-all-start = ((s32[64,1,1]{2,1,0:T(1,128)}), s32[64,1,1]{2,1,0:T(1,128)S(1)}, u32[]{:S(2)}, u32[]{:S(2)}) async-start(s32[64,1,1]{2,1,0:T(1,128)} %copy.303), calls=%async_computation | async-start | bytes 65536 | tf_op jit(solution)/shard_map/all_to_all | solution.py:102
  40.4 1.2 reduce.18
  42.8 2.9 maximum_maximum_fusion
  48.7 3.0 copy.293
  51.7 0.9 copy.294
  52.6 1.6 gather_fusion.14
  54.3 0.9 copy.291
  55.2 1.6 gather_fusion.12
  75.9 2.8 gather_fusion.13
  78.7 1.2 copy.296
  80.6 2.1 gather_fusion.7
  82.7 1.3 copy.422
  84.0 1.5 copy.281
  85.5 2.1 gather_fusion.5
  87.6 1.3 copy.423
  88.9 1.5 copy.277
  90.4 2.1 gather_fusion.3
  92.4 1.3 copy.424
  94.4 1.5 gather_fusion.1
  95.9 0.9 copy.279
  96.8 1.7 gather_fusion.4
  98.6 1.4 gather_fusion.8
  100.1 1.4 gather_fusion.18
  101.5 1.4 gather_fusion.20
  102.8 1.4 gather_fusion.24
  104.2 1.4 gather_fusion.26
  105.6 1.4 gather_fusion.6
  107.0 1.4 gather_fusion.2
  108.4 1.4 gather_fusion
  109.8 6.8 %multiply_convert_fusion.1 = (bf16[8,8,8,8,64]{4,0,3,2,1:T(8,128)(2,1)S(1)}, f32[8,8,8,8,64]{4,0,3,2,1:T(8,128)}) fusion(f32[8,8,8,8]{0,3,2,1:T(8,128)} %bitcast.539, bf16[3,3,3,64,64]{4,3,2,1,0:T(8,128)(2,1)S(1)} %copy-done, bf16[8,1,1,1,64]{4,0,3,2,1:T(8,128)(2,1)S(1)} %bitcast.601, bf16[8,1,1,8,64]{4,0,3,2,1:T(8,128)(2,1)} %bitcast.573, ...), kind=kOutput, calls=%fused_computation.34 | convolution fusion | flops 920854528 | bytes 2834432 | tf_op jit(solution)/shard_map/conv_general_dilated | solution.py:77
  117.8 1.5 scatter_custom_fusion.1
  119.8 2.1 reduce.56
  121.9 2.6 reshape.781
  124.5 10.3 %all-to-all-start.1 = ((bf16[64,2,4096]{2,1,0:T(2,128)(2,1)}), bf16[64,2,4096]{2,1,0:T(2,128)(2,1)S(1)}, u32[]{:S(2)}, u32[]{:S(2)}) async-start(bf16[64,2,4096]{2,1,0:T(2,128)(2,1)} %reshape.781), calls=%async_computation.1 | async-start | bytes 2097152 | tf_op jit(solution)/shard_map/all_to_all | solution.py:110
  134.9 26.5 %all-to-all-done.1 = bf16[64,2,4096]{2,1,0:T(2,128)(2,1)S(1)} async-done(((bf16[64,2,4096]{2,1,0:T(2,128)(2,1)}), bf16[64,2,4096]{2,1,0:T(2,128)(2,1)S(1)}, u32[]{:S(2)}, u32[]{:S(2)}) %all-to-all-start.1) | async-done | bytes 1048608 | tf_op jit(solution)/shard_map/all_to_all | solution.py:110
  161.4 3.5 reshape.782
  164.9 4.0 scatter_custom_fusion.2
  169.7 1.3 fusion.92
  171.3 1.3 gather_fusion.27
  172.6 1.2 fusion.86
  173.8 2.7 reduce.57
  176.5 1.6 reshape.783
  178.1 7.9 %all-to-all-start.2 = ((bf16[64,2,4096]{2,1,0:T(2,128)(2,1)}), bf16[64,2,4096]{2,1,0:T(2,128)(2,1)S(1)}, u32[]{:S(2)}, u32[]{:S(2)}) async-start(bf16[64,2,4096]{2,1,0:T(2,128)(2,1)} %reshape.783), calls=%async_computation.2 | async-start | bytes 2097152 | tf_op jit(solution)/shard_map/all_to_all | solution.py:117
  186.0 1.3 pad_clamp_fusion
  187.3 1.2 compare_and_fusion.1
  188.5 0.9 copy.319
  190.5 6.2 %maximum_maximum_fusion.2 = bf16[8,9,10,10,64]{4,0,3,2,1:T(8,128)(2,1)} fusion(bf16[8,1,1,1,64]{4,0,3,2,1:T(8,128)(2,1)} %bitcast.602, bf16[8,1,1,8,64]{4,0,3,2,1:T(8,128)(2,1)S(1)} %bitcast.574, bf16[8,1,1,1,64]{4,0,3,2,1:T(8,128)(2,1)} %bitcast.598, bf16[8,1,8,1,64]{4,0,3,2,1:T(8,128)(2,1)S(1)} %bitcast.576, bf16[8,1,8,8,64]{4,0,3,2,1:T(8,128)(2,1)S(1)} %bitcast.545, ...), kind=kLoop, calls=%fused_computation.91 | loop fusion | flops 7833600 | bytes 1843200 | tf_op jit(solution)/shard_map/concatenate | solution.py:37
  196.7 3.3 maximum_maximum_fusion.1
  200.9 11.7 %all-to-all-done.2 = bf16[64,2,4096]{2,1,0:T(2,128)(2,1)S(1)} async-done(((bf16[64,2,4096]{2,1,0:T(2,128)(2,1)}), bf16[64,2,4096]{2,1,0:T(2,128)(2,1)S(1)}, u32[]{:S(2)}, u32[]{:S(2)}) %all-to-all-start.2) | async-done | bytes 1048608 | tf_op jit(solution)/shard_map/all_to_all | solution.py:117
  212.6 3.5 reshape.784
  216.1 2.8 copy.406
  219.6 1.8 convolution_bitcast_fusion.1
  222.9 1.3 copy-done.3
  224.2 1.1 multiply_convert_fusion
  234.5 1.0 fusion.72
  237.1 1.0 copy-done.4
  242.8 0.9 copy-done.12
  243.8 50.9 %all-reduce.7.cloned.1.call-done = (f32[3,3,3,64,64]{4,3,2,1,0:T(8,128)}, f32[2,2,2,64,128]{4,3,0,1,2:T(8,128)}, f32[128,256]{1,0:T(8,128)}) async-done(((f32[3,3,3,64,64]{4,3,2,1,0:T(8,128)}, f32[2,2,2,64,128]{4,3,0,1,2:T(8,128)}, f32[128,256]{1,0:T(8,128)}), (f32[3,3,3,64,64]{4,3,2,1,0:T(8,128)}, f32[2,2,2,64,128]{4,3,0,1,2:T(8,128)}, f32[128,256]{1,0:T(8,128)})) %all-reduce.7.cloned.1.call-update) | async-done | bytes 835600 | tf_op jit(solution)/shard_map/psum | solution.py:145
  294.6 194.7 %all-reduce.5.cloned.1.call-done = (f32[3,3,3,64,64]{4,3,2,1,0:T(8,128)}, f32[2,2,2,64,128]{4,3,0,1,2:T(8,128)}, f32[128,256]{1,0:T(8,128)}) async-done(((f32[3,3,3,64,64]{4,3,2,1,0:T(8,128)}, f32[2,2,2,64,128]{4,3,0,1,2:T(8,128)}, f32[128,256]{1,0:T(8,128)}), (f32[3,3,3,64,64]{4,3,2,1,0:T(8,128)}, f32[2,2,2,64,128]{4,3,0,1,2:T(8,128)}, f32[128,256]{1,0:T(8,128)})) %all-reduce.5.cloned.1.call-update) | async-done | bytes 835600 | tf_op jit(solution)/shard_map/psum | solution.py:145
  489.4 1.7 copy.325
  491.1 2.2 copy.460
  (227 shorter events, 61.3 us)
Async XLA Ops:
  7.2 102.6 %copy-start = (bf16[3,3,3,64,64]{4,3,2,1,0:T(8,128)(2,1)S(1)}, bf16[3,3,3,64,64]{4,3,2,1,0:T(8,128)(2,1)}, u32[]{:S(2)}) copy-start(bf16[3,3,3,64,64]{4,3,2,1,0:T(8,128)(2,1)} %param.12) | copy-start | bytes 663556
  9.1 33.8 %collective-permute-start = (bf16[8,8,8,8,64]{4,0,3,2,1:T(8,128)(2,1)S(1)}, bf16[8,8,8,8,64]{4,0,3,2,1:T(8,128)(2,1)S(1)}, u32[]{:S(2)}, u32[]{:S(2)}) collective-permute-start(bf16[8,8,8,8,64]{4,0,3,2,1:T(8,128)(2,1)S(1)} %bitcast.503), channel_id=1, source_target_pairs={{0,1},{1,2},{2,3},{3,4},{4,5},{5,6},{6,7},{7,8},{8,9},{9,10},{10,1... | collective-permute-start | bytes 1572872 | tf_op jit(solution)/shard_map/ppermute | solution.py:16
  12.7 30.1 %collective-permute-start.1 = (bf16[8,8,8,8,64]{4,0,3,2,1:T(8,128)(2,1)S(1)}, bf16[8,8,8,8,64]{4,0,3,2,1:T(8,128)(2,1)}, u32[]{:S(2)}, u32[]{:S(2)}) collective-permute-start(bf16[8,8,8,8,64]{4,0,3,2,1:T(8,128)(2,1)S(1)} %bitcast.504), channel_id=1, source_target_pairs={{1,0},{2,1},{3,2},{4,3},{5,4},{6,5},{7,6},{8,7},{9,8},{10,9},{11,1... | collective-permute-start | bytes 1572872 | tf_op jit(solution)/shard_map/ppermute | solution.py:17
  15.3 2.3 copy-start.47
  15.6 2.0 copy-start.50
  16.3 1.3 copy-start.51
  17.6 22.8 %all-to-all-start = ((s32[64,1,1]{2,1,0:T(1,128)}), s32[64,1,1]{2,1,0:T(1,128)S(1)}, u32[]{:S(2)}, u32[]{:S(2)}) async-start(s32[64,1,1]{2,1,0:T(1,128)} %copy.303), calls=%async_computation | async-start | bytes 65536 | tf_op jit(solution)/shard_map/all_to_all | solution.py:102
  41.6 4.1 copy-start.48
  58.3 14.6 %copy-start.21 = (bf16[25,8,64]{2,0,1:T(8,128)(2,1)S(1)}, bf16[25,8,64]{2,0,1:T(8,128)(2,1)}, u32[]{:S(2)}) copy-start(bf16[25,8,64]{2,0,1:T(8,128)(2,1)} %get-tuple-element.50) | copy-start | bytes 76804
  64.9 44.9 %copy-start.6 = (bf16[8,8,8,64]{3,0,2,1:T(8,128)(2,1)}, bf16[8,8,8,64]{3,0,2,1:T(8,128)(2,1)S(1)}, u32[]{:S(2)}) copy-start(bf16[8,8,8,64]{3,0,2,1:T(8,128)(2,1)S(1)} %copy.409) | copy-start | bytes 196612
  78.7 20.0 %copy-start.1 = (bf16[8,8,8,8,64]{4,3,2,1,0:T(8,128)(2,1)}, bf16[8,8,8,8,64]{4,3,2,1,0:T(8,128)(2,1)S(1)}, u32[]{:S(2)}) copy-start(bf16[8,8,8,8,64]{4,3,2,1,0:T(8,128)(2,1)S(1)} %gather_fusion.13) | copy-start | bytes 1572868
  78.7 1.3 copy-start.20
  95.9 20.7 %copy-start.32 = (bf16[8,8,64]{2,0,1:T(8,128)(2,1)}, bf16[8,8,64]{2,0,1:T(8,128)(2,1)S(1)}, u32[]{:S(2)}) copy-start(bf16[8,8,64]{2,0,1:T(8,128)(2,1)S(1)} %copy.425) | copy-start | bytes 24580
  98.6 18.0 %copy-start.14 = (bf16[8,8,8,64]{3,0,2,1:T(8,128)(2,1)}, bf16[8,8,8,64]{3,0,2,1:T(8,128)(2,1)S(1)}, u32[]{:S(2)}) copy-start(bf16[8,8,8,64]{3,0,2,1:T(8,128)(2,1)S(1)} %copy.413) | copy-start | bytes 196612
  100.1 16.6 %copy-start.35 = (bf16[8,64]{1,0:T(8,128)(2,1)}, bf16[8,64]{1,0:T(8,128)(2,1)S(1)}, u32[]{:S(2)}) copy-start(bf16[8,64]{1,0:T(8,128)(2,1)S(1)} %gather_fusion.8) | copy-start | bytes 3076
  101.4 15.2 %copy-start.37 = (bf16[8,64]{1,0:T(8,128)(2,1)}, bf16[8,64]{1,0:T(8,128)(2,1)S(1)}, u32[]{:S(2)}) copy-start(bf16[8,64]{1,0:T(8,128)(2,1)S(1)} %gather_fusion.18) | copy-start | bytes 3076
  102.8 13.8 %copy-start.38 = (bf16[8,64]{1,0:T(8,128)(2,1)}, bf16[8,64]{1,0:T(8,128)(2,1)S(1)}, u32[]{:S(2)}) copy-start(bf16[8,64]{1,0:T(8,128)(2,1)S(1)} %gather_fusion.20) | copy-start | bytes 3076
  104.2 12.4 %copy-start.41 = (bf16[8,64]{1,0:T(8,128)(2,1)}, bf16[8,64]{1,0:T(8,128)(2,1)S(1)}, u32[]{:S(2)}) copy-start(bf16[8,64]{1,0:T(8,128)(2,1)S(1)} %gather_fusion.24) | copy-start | bytes 3076
  105.6 11.0 %copy-start.44 = (bf16[8,64]{1,0:T(8,128)(2,1)}, bf16[8,64]{1,0:T(8,128)(2,1)S(1)}, u32[]{:S(2)}) copy-start(bf16[8,64]{1,0:T(8,128)(2,1)S(1)} %gather_fusion.26) | copy-start | bytes 3076
  107.0 9.6 %copy-start.39 = (bf16[8,64]{1,0:T(8,128)(2,1)}, bf16[8,64]{1,0:T(8,128)(2,1)S(1)}, u32[]{:S(2)}) copy-start(bf16[8,64]{1,0:T(8,128)(2,1)S(1)} %gather_fusion.6) | copy-start | bytes 3076
  108.4 8.3 %copy-start.42 = (bf16[8,64]{1,0:T(8,128)(2,1)}, bf16[8,64]{1,0:T(8,128)(2,1)S(1)}, u32[]{:S(2)}) copy-start(bf16[8,64]{1,0:T(8,128)(2,1)S(1)} %gather_fusion.2) | copy-start | bytes 3076
  109.8 6.9 %copy-start.45 = (bf16[8,64]{1,0:T(8,128)(2,1)}, bf16[8,64]{1,0:T(8,128)(2,1)S(1)}, u32[]{:S(2)}) copy-start(bf16[8,64]{1,0:T(8,128)(2,1)S(1)} %gather_fusion) | copy-start | bytes 3076
  109.8 6.9 %copy-start.24 = (bf16[2,2,2,64,128]{4,3,2,1,0:T(8,128)(2,1)S(1)}, bf16[2,2,2,64,128]{4,3,2,1,0:T(8,128)(2,1)}, u32[]{:S(2)}) copy-start(bf16[2,2,2,64,128]{4,3,2,1,0:T(8,128)(2,1)} %param.13) | copy-start | bytes 393220
  116.7 1.0 copy-start.53
  117.1 0.7 copy-start.9
  121.9 12.9 %copy-start.49 = (s32[64]{0:T(128)S(1)}, s32[64]{0:T(128)}, u32[]{:S(2)}) copy-start(s32[64]{0:T(128)} %copy-done.48) | copy-start | bytes 772
  124.5 36.9 %all-to-all-start.1 = ((bf16[64,2,4096]{2,1,0:T(2,128)(2,1)}), bf16[64,2,4096]{2,1,0:T(2,128)(2,1)S(1)}, u32[]{:S(2)}, u32[]{:S(2)}) async-start(bf16[64,2,4096]{2,1,0:T(2,128)(2,1)} %reshape.781), calls=%async_computation.1 | async-start | bytes 2097152 | tf_op jit(solution)/shard_map/all_to_all | solution.py:110
  134.9 34.8 %copy-start.34 = (bf16[128,256]{1,0:T(8,128)(2,1)S(1)}, bf16[128,256]{1,0:T(8,128)(2,1)}, u32[]{:S(2)}) copy-start(bf16[128,256]{1,0:T(8,128)(2,1)} %param.14) | copy-start | bytes 196612
  169.0 0.6 copy-start.16
  176.4 14.0 %copy-start.7 = (bf16[8,8,8,64]{3,0,2,1:T(8,128)(2,1)S(1)}, bf16[8,8,8,64]{3,0,2,1:T(8,128)(2,1)}, u32[]{:S(2)}) copy-start(bf16[8,8,8,64]{3,0,2,1:T(8,128)(2,1)} %copy-done.6) | copy-start | bytes 196612
  176.5 14.0 %copy-start.8 = (bf16[8,8,8,64]{3,0,2,1:T(8,128)(2,1)S(1)}, bf16[8,8,8,64]{3,0,2,1:T(8,128)(2,1)}, u32[]{:S(2)}) copy-start(bf16[8,8,8,64]{3,0,2,1:T(8,128)(2,1)} %copy.412) | copy-start | bytes 196612
  176.5 14.0 %copy-start.13 = (bf16[8,8,8,64]{3,0,2,1:T(8,128)(2,1)S(1)}, bf16[8,8,8,64]{3,0,2,1:T(8,128)(2,1)}, u32[]{:S(2)}) copy-start(bf16[8,8,8,64]{3,0,2,1:T(8,128)(2,1)} %copy.408) | copy-start | bytes 196612
  176.5 13.9 %copy-start.22 = (bf16[8,8,64]{2,0,1:T(8,128)(2,1)S(1)}, bf16[8,8,64]{2,0,1:T(8,128)(2,1)}, u32[]{:S(2)}) copy-start(bf16[8,8,64]{2,0,1:T(8,128)(2,1)} %copy.420) | copy-start | bytes 24580
  176.5 13.9 %copy-start.23 = (bf16[8,8,64]{2,0,1:T(8,128)(2,1)S(1)}, bf16[8,8,64]{2,0,1:T(8,128)(2,1)}, u32[]{:S(2)}) copy-start(bf16[8,8,64]{2,0,1:T(8,128)(2,1)} %copy.421) | copy-start | bytes 24580
  176.5 13.9 %copy-start.27 = (bf16[8,8,64]{2,0,1:T(8,128)(2,1)S(1)}, bf16[8,8,64]{2,0,1:T(8,128)(2,1)}, u32[]{:S(2)}) copy-start(bf16[8,8,64]{2,0,1:T(8,128)(2,1)} %copy.414) | copy-start | bytes 24580
  176.5 13.9 %copy-start.28 = (bf16[8,8,64]{2,0,1:T(8,128)(2,1)S(1)}, bf16[8,8,64]{2,0,1:T(8,128)(2,1)}, u32[]{:S(2)}) copy-start(bf16[8,8,64]{2,0,1:T(8,128)(2,1)} %copy.415) | copy-start | bytes 24580
  178.1 34.5 %all-to-all-start.2 = ((bf16[64,2,4096]{2,1,0:T(2,128)(2,1)}), bf16[64,2,4096]{2,1,0:T(2,128)(2,1)S(1)}, u32[]{:S(2)}, u32[]{:S(2)}) async-start(bf16[64,2,4096]{2,1,0:T(2,128)(2,1)} %reshape.783), calls=%async_computation.2 | async-start | bytes 2097152 | tf_op jit(solution)/shard_map/all_to_all | solution.py:117
  186.0 108.6 %all-reduce.7.cloned.1.call-start = ((), (), s32[]{:S(2)}) async-start(), calls=%async_computation.4 | async-start | bytes 2555904 | tf_op jit(solution)/shard_map/psum | solution.py:145
  189.4 7.2 %copy-start.15 = (bf16[8,8,8,64]{3,0,2,1:T(8,128)(2,1)S(1)}, bf16[8,8,8,64]{3,0,2,1:T(8,128)(2,1)}, u32[]{:S(2)}) copy-start(bf16[8,8,8,64]{3,0,2,1:T(8,128)(2,1)} %copy-done.14) | copy-start | bytes 196612
  189.4 7.2 %copy-start.29 = (bf16[8,8,64]{2,0,1:T(8,128)(2,1)S(1)}, bf16[8,8,64]{2,0,1:T(8,128)(2,1)}, u32[]{:S(2)}) copy-start(bf16[8,8,64]{2,0,1:T(8,128)(2,1)} %copy.422) | copy-start | bytes 24580
  189.4 7.2 %copy-start.30 = (bf16[8,8,64]{2,0,1:T(8,128)(2,1)S(1)}, bf16[8,8,64]{2,0,1:T(8,128)(2,1)}, u32[]{:S(2)}) copy-start(bf16[8,8,64]{2,0,1:T(8,128)(2,1)} %copy.423) | copy-start | bytes 24580
  189.4 7.2 %copy-start.31 = (bf16[8,8,64]{2,0,1:T(8,128)(2,1)S(1)}, bf16[8,8,64]{2,0,1:T(8,128)(2,1)}, u32[]{:S(2)}) copy-start(bf16[8,8,64]{2,0,1:T(8,128)(2,1)} %copy.424) | copy-start | bytes 24580
  189.5 7.2 %copy-start.33 = (bf16[8,8,64]{2,0,1:T(8,128)(2,1)S(1)}, bf16[8,8,64]{2,0,1:T(8,128)(2,1)}, u32[]{:S(2)}) copy-start(bf16[8,8,64]{2,0,1:T(8,128)(2,1)} %copy-done.32) | copy-start | bytes 24580
  189.5 7.2 %copy-start.36 = (bf16[8,64]{1,0:T(8,128)(2,1)S(1)}, bf16[8,64]{1,0:T(8,128)(2,1)}, u32[]{:S(2)}) copy-start(bf16[8,64]{1,0:T(8,128)(2,1)} %copy-done.35) | copy-start | bytes 3076
  189.5 7.2 %copy-start.40 = (bf16[8,64]{1,0:T(8,128)(2,1)S(1)}, bf16[8,64]{1,0:T(8,128)(2,1)}, u32[]{:S(2)}) copy-start(bf16[8,64]{1,0:T(8,128)(2,1)} %copy-done.39) | copy-start | bytes 3076
  189.5 7.2 %copy-start.43 = (bf16[8,64]{1,0:T(8,128)(2,1)S(1)}, bf16[8,64]{1,0:T(8,128)(2,1)}, u32[]{:S(2)}) copy-start(bf16[8,64]{1,0:T(8,128)(2,1)} %copy-done.42) | copy-start | bytes 3076
  189.5 7.2 %copy-start.46 = (bf16[8,64]{1,0:T(8,128)(2,1)S(1)}, bf16[8,64]{1,0:T(8,128)(2,1)}, u32[]{:S(2)}) copy-start(bf16[8,64]{1,0:T(8,128)(2,1)} %copy-done.45) | copy-start | bytes 3076
  196.7 3.3 copy-start.17
  216.1 3.5 copy-start.10
  216.1 3.5 copy-start.52
  219.6 1.8 copy-start.25
  222.6 1.6 copy-start.3
  222.6 1.6 copy-start.11
  224.2 1.5 copy-start.5
  231.4 1.2 copy-start.2
  231.4 1.3 copy-start.19
  233.6 1.0 copy-start.18
  236.6 1.5 copy-start.4
  242.8 0.9 copy-start.12
  243.7 245.7 %all-reduce.5.cloned.1.call-start = ((), (), s32[]{:S(2)}) async-start(), calls=%async_computation.3 | async-start | bytes 2555904 | tf_op jit(solution)/shard_map/psum | solution.py:145
  489.4 3.9 copy-start.26
Sparse Core Ops, SparseCore 0:
  243.8 50.7 all-reduce.6
  298.3 191.0 all-reduce.4
